TPU v7x, 32 devices: a whole 2x2x4 slice. The times are simulated.
32 devices in a mesh: db: 8 (over y, x, core), pb: 4 (over z).
Axes of the slice: x: 2, y: 2, z: 4, core: 2. Of those that a mesh axis runs over, the one named last changes fastest.
Arguments:
- query_maps: bfloat16 [32, 256, 256], P(('db', 'pb')), may hold values from -6 to 6
- database: bfloat16 [1024, 256, 256], P(('db', 'pb')), may hold values from -6 to 6
- shortlist: int32 [32, 128], P(('db', 'pb')), may hold values from 0 to 1023, as said below
- kernel_query: bfloat16 [3, 3], replicated, may hold values from -1.5 to 1.5
- kernel_db: bfloat16 [3, 3], replicated, may hold values from -1.5 to 1.5
Outputs:
- scores: float32 [32, 128], P(('db', 'pb'))
- top_scores: float32 [32, 100], P(('db', 'pb'))
Inputs may be any that keep to these rules, and one draw needn't show every extreme that they name: Within one query the ids are distinct. Among the 128 shortlist entries of the query held by device q (query q), at most 8 lie in any one shard of images (ids s * 32 to (s + 1) * 32 - 1), and some shard holds exactly 8 of them for every device.
All inputs are finite; a program needn't handle non-finite values.
Results may differ from a plain program's by a relative error of at most 0.0003.
Values may be sent and summed in bfloat16 or wider, within the bound.
A program may use at most 128 MiB of HBM per device.

v0:
```python
import math
import jax
import jax.numpy as jnp
from jax import lax
from jax.sharding import PartitionSpec as P

GRID = 16
TOPK = 100
epsilon = 1e-06
score_scale = 8.0


def unit_maps(maps):
    values = maps.astype(jnp.float32)
    squares = jnp.sum(values * values, axis=1, keepdims=True)
    return (values * lax.rsqrt(squares + epsilon)).astype(jnp.bfloat16)


def conv_matrix(kernel):
    cell_count = GRID * GRID
    cell_index = jnp.arange(cell_count)
    row_out = (cell_index // GRID)[:, None]
    col_out = (cell_index % GRID)[:, None]
    row_in = (cell_index // GRID)[None, :]
    col_in = (cell_index % GRID)[None, :]
    weights = kernel.astype(jnp.float32)
    matrix = jnp.zeros((cell_count, cell_count), jnp.float32)
    for i in range(3):
        for j in range(3):
            hit = (row_in == row_out + i - 1) & (col_in == col_out + j - 1)
            matrix = matrix + weights[i, j] * hit.astype(jnp.float32)
    return matrix.astype(jnp.bfloat16)


def finish_pairs(correlation, conv_query, conv_db):
    rectified = jnp.maximum(correlation, 0.0).astype(jnp.bfloat16)
    filtered = jnp.einsum("qa,nab->nqb", conv_query, rectified, preferred_element_type=jnp.float32)
    filtered = filtered + jnp.einsum(
        "nqa,ba->nqb", rectified, conv_db, preferred_element_type=jnp.float32
    )
    return score_scale * jnp.mean(jnp.max(filtered, axis=1), axis=-1)


def shard_scores(gathered, slots, db_unit, conv_query, conv_db):
    source_count, width = slots.shape
    per_query = gathered.shape[0] // source_count
    grouped = gathered.reshape(source_count, per_query, gathered.shape[1], gathered.shape[2])
    step_size = math.gcd(source_count, max(1, 32 // width))

    def score_block(start):
        slot_block = lax.dynamic_slice_in_dim(slots, start, step_size, 0)
        group_block = lax.dynamic_slice_in_dim(grouped, start, step_size, 0)
        images = db_unit[slot_block]
        correlation = jnp.einsum(
            "scq,skcd->skqd", group_block[:, 0], images, preferred_element_type=jnp.float32
        )
        correlation = correlation.reshape(
            step_size * width, correlation.shape[-2], correlation.shape[-1]
        )
        return finish_pairs(correlation, conv_query, conv_db)

    starts = jnp.arange(source_count // step_size, dtype=jnp.int32) * step_size
    return lax.map(score_block, starts).reshape(source_count, width)


def body(query_maps, database, shortlist, kernel_query, kernel_db):
    query_unit = unit_maps(query_maps)
    db_unit = unit_maps(database)
    conv_query = conv_matrix(kernel_query)
    conv_db = conv_matrix(kernel_db)
    db_count = lax.axis_size("db")
    pb_count = lax.axis_size("pb")
    shard_count = db_count * pb_count
    per_query = query_maps.shape[0]
    cand_count = shortlist.shape[1]
    image_count = database.shape[0]
    flat_ids = shortlist.reshape(-1)
    row_count = flat_ids.shape[0]
    capacity = 2 * row_count // shard_count
    shard_of = flat_ids // image_count
    slot_of = flat_ids % image_count
    one_hot = (shard_of[:, None] == jnp.arange(shard_count, dtype=jnp.int32)[None, :]).astype(
        jnp.int32
    )
    bucket_pos = jnp.sum(jnp.cumsum(one_hot, axis=0) * one_hot, axis=1) - 1
    row_ids = jnp.arange(row_count, dtype=jnp.int32)
    query_of = row_ids // cand_count
    empty = jnp.zeros((shard_count, capacity), jnp.int32)
    send_slot = empty.at[shard_of, bucket_pos].set(slot_of)
    send_query = empty.at[shard_of, bucket_pos].set(query_of)
    requests = jnp.stack([send_slot, send_query])
    gathered = lax.all_gather(query_unit, ("db", "pb"), axis=0, tiled=True)
    found = shard_scores(
        gathered,
        lax.all_to_all(requests, ("db", "pb"), split_axis=1, concat_axis=1, tiled=True)[0],
        db_unit,
        conv_query,
        conv_db,
    )
    returned = lax.all_to_all(found, ("db", "pb"), split_axis=0, concat_axis=0, tiled=True)
    scores = returned[shard_of, bucket_pos].reshape(per_query, cand_count)
    top_scores = lax.top_k(scores, TOPK)[0]
    return (scores, top_scores)


def solution(mesh):
    in_specs = (
        P(("db", "pb"), None, None),
        P(("db", "pb"), None, None),
        P(("db", "pb"), None),
        P(),
        P(),
    )
    out_specs = (P(("db", "pb"), None), P(("db", "pb"), None))
    return jax.shard_map(body, mesh=mesh, in_specs=in_specs, out_specs=out_specs, check_vma=False)
```

profile of v0, /device:TPU:0, one launch (start us, length us, event | category | flops | bytes accessed | tf_op | source)
XLA Modules:
  0.0 317.0 jit_solution(1332410492687568349)
XLA Ops:
  11.6 6.4 %scatter_fusion = s32[32,8]{0,1:T(8,128)S(1)} fusion(s32[32,8]{0,1:T(8,128)S(1)} %broadcast_in_dim.11.clone.1, s32[128]{0:T(128)S(1)} %fusion.60, s32[128]{0:T(128)S(1)} %get-tuple-element.427), kind=kCustom, calls=%fused_computation.2 | custom fusion | bytes 2560 | tf_op jit(solution)/shard_map/scatter | solution.py:89
  18.1 6.4 %scatter_fusion.1 = s32[32,8]{0,1:T(8,128)S(1)} fusion(s32[32,8]{0,1:T(8,128)S(1)} %broadcast_in_dim.11.clone, s32[128]{0:T(128)S(1)} %fusion.60, s32[128]{0:T(128)S(1)} %and_select_fusion.2), kind=kCustom, calls=%fused_computation.3 | custom fusion | bytes 2560 | tf_op jit(solution)/shard_map/scatter | solution.py:90
  25.2 7.3 %all-to-all-start = ((s32[2,32,8]{2,0,1:T(2,128)}), s32[2,32,8]{2,0,1:T(2,128)S(1)}, u32[]{:S(2)}, u32[]{:S(2)}) async-start(s32[2,32,8]{2,0,1:T(2,128)} %copy.23), calls=%async_computation | async-start | bytes 65536 | tf_op jit(solution)/shard_map/all_to_all | solution.py:95
  42.2 33.2 %all-gather.2.cloned.1.call-done = bf16[32,256,256]{2,1,0:T(8,128)(2,1)} async-done(((bf16[1,256,256]{2,1,0:T(8,128)(2,1)}), bf16[32,256,256]{2,1,0:T(8,128)(2,1)}) %all-gather.2.cloned.1.call-update) | async-done | bytes 4194320 | tf_op jit(solution)/shard_map/all_gather | solution.py:92
  75.4 220.3 %while.14 = (s32[]{:T(128)}, f32[8,32]{1,0:T(8,128)S(1)}, s32[8]{0:T(128)S(1)}, s32[32,8]{1,0:T(8,128)S(1)}, bf16[32,256,256]{2,1,0:T(8,128)(2,1)}, /*index=5*/b...) while((s32[]{:T(128)}, f32[8,32]{1,0:T(8,128)S(1)}, ...), condition=%wide.region_9.10_spmd.clone.clone, body=%wide.region_6.9_spmd.clone.clone.sunk | while | flops 3233940480 | bytes 42551080 | solution.py:63
  77.8 5.0 %gather_fusion = bf16[32,256,256]{2,1,0:T(8,128)(2,1)} fusion(bf16[32,256,256]{2,1,0:T(8,128)(2,1)} %get-tuple-element.688, s32[1024]{0:T(1024)S(1)} %pad_clamp_fusion.2), kind=kCustom, calls=%fused_computation.clone.clone.clone.1 | custom fusion | bytes 8388736 | tf_op jit(solution)/shard_map/while/body/eval_jaxpr/gather | solution.py:53
  82.7 4.0 %maximum_convert_fusion.2 = bf16[4,8,256,256]{3,2,1,0:T(8,128)(2,1)S(1)} fusion(bf16[4,8,256,256]{3,2,1,0:T(8,128)(2,1)} %bitcast.126, bf16[32,1,256,256]{3,2,0,1:T(8,128)(2,1)} %get-tuple-element.689, s32[]{:T(128)S(6)} %select_n.224), kind=kOutput, calls=%fused_computation.8.clone.1 | convolution fusion | flops 1077936128 | bytes 8912900 | tf_op jit(solution)/shard_map/while/body/eval_jaxpr/scq,skcd->skqd/dot_general | solution.py:54
  86.8 7.3 %fusion.81 = f32[32,256,256]{1,2,0:T(8,128)S(1)} fusion(bf16[32,256,256]{1,2,0:T(8,128)(2,1)S(1)} %bitcast.124, f32[]{:T(128)} %get-tuple-element.704, f32[]{:T(128)} %get-tuple-element.701, f32[]{:T(128)} %get-tuple-element.699, f32[]{:T(128)} %get-tuple-element.697, f32[]{:T(128)} %get-tuple-element.695, f32[]{:T(128)} %get-tuple-element.694, ...), kind=kOutput, calls=%fused_computation.23.clone.1 | convolution fusion | flops 1075904512 | bytes 12589092 | tf_op jit(solution)/shard_map/while/body/eval_jaxpr/qa,nab->nqb/dot_general | solution.py:37
  94.1 8.6 %fusion.82 = f32[32,256]{1,0:T(8,128)S(1)} fusion(f32[32,256,256]{1,2,0:T(8,128)S(1)} %fusion.81, bf16[32,256,256]{1,2,0:T(8,128)(2,1)S(1)} %bitcast.125, f32[]{:T(128)} %get-tuple-element.713, f32[]{:T(128)} %get-tuple-element.712, f32[]{:T(128)} %get-tuple-element.711, f32[]{:T(128)} %get-tuple-element.710, f32[]{:T(128)} %get-tuple-element.709, ...), kind=kOutput, calls=%fused_computation.7.clone.1 | convolution fusion | flops 1080090624 | bytes 12621860 | tf_op jit(solution)/shard_map/while/body/eval_jaxpr/nqa,ba->nqb/dot_general | solution.py:38
  105.3 5.0 %gather_fusion = bf16[32,256,256]{2,1,0:T(8,128)(2,1)} fusion(bf16[32,256,256]{2,1,0:T(8,128)(2,1)} %get-tuple-element.688, s32[1024]{0:T(1024)S(1)} %pad_clamp_fusion.2), kind=kCustom, calls=%fused_computation.clone.clone.clone.1 | custom fusion | bytes 8388736 | tf_op jit(solution)/shard_map/while/body/eval_jaxpr/gather | solution.py:53
  114.3 7.3 %fusion.81 = f32[32,256,256]{1,2,0:T(8,128)S(1)} fusion(bf16[32,256,256]{1,2,0:T(8,128)(2,1)S(1)} %bitcast.124, f32[]{:T(128)} %get-tuple-element.704, f32[]{:T(128)} %get-tuple-element.701, f32[]{:T(128)} %get-tuple-element.699, f32[]{:T(128)} %get-tuple-element.697, f32[]{:T(128)} %get-tuple-element.695, f32[]{:T(128)} %get-tuple-element.694, ...), kind=kOutput, calls=%fused_computation.23.clone.1 | convolution fusion | flops 1075904512 | bytes 12589092 | tf_op jit(solution)/shard_map/while/body/eval_jaxpr/qa,nab->nqb/dot_general | solution.py:37
  121.6 8.6 %fusion.82 = f32[32,256]{1,0:T(8,128)S(1)} fusion(f32[32,256,256]{1,2,0:T(8,128)S(1)} %fusion.81, bf16[32,256,256]{1,2,0:T(8,128)(2,1)S(1)} %bitcast.125, f32[]{:T(128)} %get-tuple-element.713, f32[]{:T(128)} %get-tuple-element.712, f32[]{:T(128)} %get-tuple-element.711, f32[]{:T(128)} %get-tuple-element.710, f32[]{:T(128)} %get-tuple-element.709, ...), kind=kOutput, calls=%fused_computation.7.clone.1 | convolution fusion | flops 1080090624 | bytes 12621860 | tf_op jit(solution)/shard_map/while/body/eval_jaxpr/nqa,ba->nqb/dot_general | solution.py:38
  132.8 5.0 %gather_fusion = bf16[32,256,256]{2,1,0:T(8,128)(2,1)} fusion(bf16[32,256,256]{2,1,0:T(8,128)(2,1)} %get-tuple-element.688, s32[1024]{0:T(1024)S(1)} %pad_clamp_fusion.2), kind=kCustom, calls=%fused_computation.clone.clone.clone.1 | custom fusion | bytes 8388736 | tf_op jit(solution)/shard_map/while/body/eval_jaxpr/gather | solution.py:53
  141.8 7.3 %fusion.81 = f32[32,256,256]{1,2,0:T(8,128)S(1)} fusion(bf16[32,256,256]{1,2,0:T(8,128)(2,1)S(1)} %bitcast.124, f32[]{:T(128)} %get-tuple-element.704, f32[]{:T(128)} %get-tuple-element.701, f32[]{:T(128)} %get-tuple-element.699, f32[]{:T(128)} %get-tuple-element.697, f32[]{:T(128)} %get-tuple-element.695, f32[]{:T(128)} %get-tuple-element.694, ...), kind=kOutput, calls=%fused_computation.23.clone.1 | convolution fusion | flops 1075904512 | bytes 12589092 | tf_op jit(solution)/shard_map/while/body/eval_jaxpr/qa,nab->nqb/dot_general | solution.py:37
  149.2 8.6 %fusion.82 = f32[32,256]{1,0:T(8,128)S(1)} fusion(f32[32,256,256]{1,2,0:T(8,128)S(1)} %fusion.81, bf16[32,256,256]{1,2,0:T(8,128)(2,1)S(1)} %bitcast.125, f32[]{:T(128)} %get-tuple-element.713, f32[]{:T(128)} %get-tuple-element.712, f32[]{:T(128)} %get-tuple-element.711, f32[]{:T(128)} %get-tuple-element.710, f32[]{:T(128)} %get-tuple-element.709, ...), kind=kOutput, calls=%fused_computation.7.clone.1 | convolution fusion | flops 1080090624 | bytes 12621860 | tf_op jit(solution)/shard_map/while/body/eval_jaxpr/nqa,ba->nqb/dot_general | solution.py:38
  160.4 5.0 %gather_fusion = bf16[32,256,256]{2,1,0:T(8,128)(2,1)} fusion(bf16[32,256,256]{2,1,0:T(8,128)(2,1)} %get-tuple-element.688, s32[1024]{0:T(1024)S(1)} %pad_clamp_fusion.2), kind=kCustom, calls=%fused_computation.clone.clone.clone.1 | custom fusion | bytes 8388736 | tf_op jit(solution)/shard_map/while/body/eval_jaxpr/gather | solution.py:53
  169.4 7.3 %fusion.81 = f32[32,256,256]{1,2,0:T(8,128)S(1)} fusion(bf16[32,256,256]{1,2,0:T(8,128)(2,1)S(1)} %bitcast.124, f32[]{:T(128)} %get-tuple-element.704, f32[]{:T(128)} %get-tuple-element.701, f32[]{:T(128)} %get-tuple-element.699, f32[]{:T(128)} %get-tuple-element.697, f32[]{:T(128)} %get-tuple-element.695, f32[]{:T(128)} %get-tuple-element.694, ...), kind=kOutput, calls=%fused_computation.23.clone.1 | convolution fusion | flops 1075904512 | bytes 12589092 | tf_op jit(solution)/shard_map/while/body/eval_jaxpr/qa,nab->nqb/dot_general | solution.py:37
  176.7 8.6 %fusion.82 = f32[32,256]{1,0:T(8,128)S(1)} fusion(f32[32,256,256]{1,2,0:T(8,128)S(1)} %fusion.81, bf16[32,256,256]{1,2,0:T(8,128)(2,1)S(1)} %bitcast.125, f32[]{:T(128)} %get-tuple-element.713, f32[]{:T(128)} %get-tuple-element.712, f32[]{:T(128)} %get-tuple-element.711, f32[]{:T(128)} %get-tuple-element.710, f32[]{:T(128)} %get-tuple-element.709, ...), kind=kOutput, calls=%fused_computation.7.clone.1 | convolution fusion | flops 1080090624 | bytes 12621860 | tf_op jit(solution)/shard_map/while/body/eval_jaxpr/nqa,ba->nqb/dot_general | solution.py:38
  187.9 5.0 %gather_fusion = bf16[32,256,256]{2,1,0:T(8,128)(2,1)} fusion(bf16[32,256,256]{2,1,0:T(8,128)(2,1)} %get-tuple-element.688, s32[1024]{0:T(1024)S(1)} %pad_clamp_fusion.2), kind=kCustom, calls=%fused_computation.clone.clone.clone.1 | custom fusion | bytes 8388736 | tf_op jit(solution)/shard_map/while/body/eval_jaxpr/gather | solution.py:53
  192.9 4.0 %maximum_convert_fusion.2 = bf16[4,8,256,256]{3,2,1,0:T(8,128)(2,1)S(1)} fusion(bf16[4,8,256,256]{3,2,1,0:T(8,128)(2,1)} %bitcast.126, bf16[32,1,256,256]{3,2,0,1:T(8,128)(2,1)} %get-tuple-element.689, s32[]{:T(128)S(6)} %select_n.224), kind=kOutput, calls=%fused_computation.8.clone.1 | convolution fusion | flops 1077936128 | bytes 8912900 | tf_op jit(solution)/shard_map/while/body/eval_jaxpr/scq,skcd->skqd/dot_general | solution.py:54
  196.9 7.3 %fusion.81 = f32[32,256,256]{1,2,0:T(8,128)S(1)} fusion(bf16[32,256,256]{1,2,0:T(8,128)(2,1)S(1)} %bitcast.124, f32[]{:T(128)} %get-tuple-element.704, f32[]{:T(128)} %get-tuple-element.701, f32[]{:T(128)} %get-tuple-element.699, f32[]{:T(128)} %get-tuple-element.697, f32[]{:T(128)} %get-tuple-element.695, f32[]{:T(128)} %get-tuple-element.694, ...), kind=kOutput, calls=%fused_computation.23.clone.1 | convolution fusion | flops 1075904512 | bytes 12589092 | tf_op jit(solution)/shard_map/while/body/eval_jaxpr/qa,nab->nqb/dot_general | solution.py:37
  204.3 8.6 %fusion.82 = f32[32,256]{1,0:T(8,128)S(1)} fusion(f32[32,256,256]{1,2,0:T(8,128)S(1)} %fusion.81, bf16[32,256,256]{1,2,0:T(8,128)(2,1)S(1)} %bitcast.125, f32[]{:T(128)} %get-tuple-element.713, f32[]{:T(128)} %get-tuple-element.712, f32[]{:T(128)} %get-tuple-element.711, f32[]{:T(128)} %get-tuple-element.710, f32[]{:T(128)} %get-tuple-element.709, ...), kind=kOutput, calls=%fused_computation.7.clone.1 | convolution fusion | flops 1080090624 | bytes 12621860 | tf_op jit(solution)/shard_map/while/body/eval_jaxpr/nqa,ba->nqb/dot_general | solution.py:38
  215.5 5.0 %gather_fusion = bf16[32,256,256]{2,1,0:T(8,128)(2,1)} fusion(bf16[32,256,256]{2,1,0:T(8,128)(2,1)} %get-tuple-element.688, s32[1024]{0:T(1024)S(1)} %pad_clamp_fusion.2), kind=kCustom, calls=%fused_computation.clone.clone.clone.1 | custom fusion | bytes 8388736 | tf_op jit(solution)/shard_map/while/body/eval_jaxpr/gather | solution.py:53
  224.5 7.3 %fusion.81 = f32[32,256,256]{1,2,0:T(8,128)S(1)} fusion(bf16[32,256,256]{1,2,0:T(8,128)(2,1)S(1)} %bitcast.124, f32[]{:T(128)} %get-tuple-element.704, f32[]{:T(128)} %get-tuple-element.701, f32[]{:T(128)} %get-tuple-element.699, f32[]{:T(128)} %get-tuple-element.697, f32[]{:T(128)} %get-tuple-element.695, f32[]{:T(128)} %get-tuple-element.694, ...), kind=kOutput, calls=%fused_computation.23.clone.1 | convolution fusion | flops 1075904512 | bytes 12589092 | tf_op jit(solution)/shard_map/while/body/eval_jaxpr/qa,nab->nqb/dot_general | solution.py:37
  231.8 8.6 %fusion.82 = f32[32,256]{1,0:T(8,128)S(1)} fusion(f32[32,256,256]{1,2,0:T(8,128)S(1)} %fusion.81, bf16[32,256,256]{1,2,0:T(8,128)(2,1)S(1)} %bitcast.125, f32[]{:T(128)} %get-tuple-element.713, f32[]{:T(128)} %get-tuple-element.712, f32[]{:T(128)} %get-tuple-element.711, f32[]{:T(128)} %get-tuple-element.710, f32[]{:T(128)} %get-tuple-element.709, ...), kind=kOutput, calls=%fused_computation.7.clone.1 | convolution fusion | flops 1080090624 | bytes 12621860 | tf_op jit(solution)/shard_map/while/body/eval_jaxpr/nqa,ba->nqb/dot_general | solution.py:38
  243.0 5.0 %gather_fusion = bf16[32,256,256]{2,1,0:T(8,128)(2,1)} fusion(bf16[32,256,256]{2,1,0:T(8,128)(2,1)} %get-tuple-element.688, s32[1024]{0:T(1024)S(1)} %pad_clamp_fusion.2), kind=kCustom, calls=%fused_computation.clone.clone.clone.1 | custom fusion | bytes 8388736 | tf_op jit(solution)/shard_map/while/body/eval_jaxpr/gather | solution.py:53
  252.0 7.3 %fusion.81 = f32[32,256,256]{1,2,0:T(8,128)S(1)} fusion(bf16[32,256,256]{1,2,0:T(8,128)(2,1)S(1)} %bitcast.124, f32[]{:T(128)} %get-tuple-element.704, f32[]{:T(128)} %get-tuple-element.701, f32[]{:T(128)} %get-tuple-element.699, f32[]{:T(128)} %get-tuple-element.697, f32[]{:T(128)} %get-tuple-element.695, f32[]{:T(128)} %get-tuple-element.694, ...), kind=kOutput, calls=%fused_computation.23.clone.1 | convolution fusion | flops 1075904512 | bytes 12589092 | tf_op jit(solution)/shard_map/while/body/eval_jaxpr/qa,nab->nqb/dot_general | solution.py:37
  259.4 8.6 %fusion.82 = f32[32,256]{1,0:T(8,128)S(1)} fusion(f32[32,256,256]{1,2,0:T(8,128)S(1)} %fusion.81, bf16[32,256,256]{1,2,0:T(8,128)(2,1)S(1)} %bitcast.125, f32[]{:T(128)} %get-tuple-element.713, f32[]{:T(128)} %get-tuple-element.712, f32[]{:T(128)} %get-tuple-element.711, f32[]{:T(128)} %get-tuple-element.710, f32[]{:T(128)} %get-tuple-element.709, ...), kind=kOutput, calls=%fused_computation.7.clone.1 | convolution fusion | flops 1080090624 | bytes 12621860 | tf_op jit(solution)/shard_map/while/body/eval_jaxpr/nqa,ba->nqb/dot_general | solution.py:38
  270.6 5.0 %gather_fusion = bf16[32,256,256]{2,1,0:T(8,128)(2,1)} fusion(bf16[32,256,256]{2,1,0:T(8,128)(2,1)} %get-tuple-element.688, s32[1024]{0:T(1024)S(1)} %pad_clamp_fusion.2), kind=kCustom, calls=%fused_computation.clone.clone.clone.1 | custom fusion | bytes 8388736 | tf_op jit(solution)/shard_map/while/body/eval_jaxpr/gather | solution.py:53
  279.6 7.3 %fusion.81 = f32[32,256,256]{1,2,0:T(8,128)S(1)} fusion(bf16[32,256,256]{1,2,0:T(8,128)(2,1)S(1)} %bitcast.124, f32[]{:T(128)} %get-tuple-element.704, f32[]{:T(128)} %get-tuple-element.701, f32[]{:T(128)} %get-tuple-element.699, f32[]{:T(128)} %get-tuple-element.697, f32[]{:T(128)} %get-tuple-element.695, f32[]{:T(128)} %get-tuple-element.694, ...), kind=kOutput, calls=%fused_computation.23.clone.1 | convolution fusion | flops 1075904512 | bytes 12589092 | tf_op jit(solution)/shard_map/while/body/eval_jaxpr/qa,nab->nqb/dot_general | solution.py:37
  286.9 8.6 %fusion.82 = f32[32,256]{1,0:T(8,128)S(1)} fusion(f32[32,256,256]{1,2,0:T(8,128)S(1)} %fusion.81, bf16[32,256,256]{1,2,0:T(8,128)(2,1)S(1)} %bitcast.125, f32[]{:T(128)} %get-tuple-element.713, f32[]{:T(128)} %get-tuple-element.712, f32[]{:T(128)} %get-tuple-element.711, f32[]{:T(128)} %get-tuple-element.710, f32[]{:T(128)} %get-tuple-element.709, ...), kind=kOutput, calls=%fused_computation.7.clone.1 | convolution fusion | flops 1080090624 | bytes 12621860 | tf_op jit(solution)/shard_map/while/body/eval_jaxpr/nqa,ba->nqb/dot_general | solution.py:38
  295.8 10.4 %all_to_all.17 = f32[32,1,8]{2,1,0:T(1,128)S(1)} all-to-all(f32[32,1,8]{2,1,0:T(1,128)S(1)} %bitcast.131), channel_id=1, replica_groups=mesh['db'=8,'pb'=4] {'db','pb'}, dimensions={0} | all-to-all | bytes 2048 | tf_op jit(solution)/shard_map/all_to_all | solution.py:100
  (98 shorter events, 49.3 us)
Async XLA Ops:
  7.2 68.2 %all-gather.2.cloned.1.call-start = ((), (), s32[]{:S(2)}) async-start(), calls=%async_computation.2 | async-start | bytes 4325376 | tf_op jit(solution)/shard_map/all_gather | solution.py:92
  25.2 16.9 %all-to-all-start = ((s32[2,32,8]{2,0,1:T(2,128)}), s32[2,32,8]{2,0,1:T(2,128)S(1)}, u32[]{:S(2)}, u32[]{:S(2)}) async-start(s32[2,32,8]{2,0,1:T(2,128)} %copy.23), calls=%async_computation | async-start | bytes 65536 | tf_op jit(solution)/shard_map/all_to_all | solution.py:95
  32.5 6.5 %copy-start = (bf16[32,256,256]{2,1,0:T(8,128)(2,1)S(1)}, bf16[32,256,256]{2,1,0:T(8,128)(2,1)}, u32[]{:S(2)}) copy-start(bf16[32,256,256]{2,1,0:T(8,128)(2,1)} %param.8) | copy-start | bytes 12582916
  307.5 2.7 copy-start.1
Sparse Core Ops, SparseCore 0:
  11.0 64.3 all-gather.1
where the time goes:
time: 319 us; the launch traced here: 317 us
  matrix products  160 us (50%)
  local copies, waits for them, and re-layouts  63.6 us (20%)
  waiting for transfers between devices  33.2 us (10%)
  other arithmetic  14.3 us (4%)
  between operations  14.2 us (4%)
  loops' own time  14 us (4%)
  blocking collectives  10.4 us (3%)
  starting transfers between devices  7.36 us (2%)
    dot_general x8, matrix products, finish_pairs(): jnp.einsum('nqa,ba->nqb', rectified, conv_db, preferred_element_type=jnp....  69.1 us
    dot_general x8, matrix products, finish_pairs(): jnp.einsum('qa,nab->nqb', conv_query, rectified, preferred_element_type=j...  58.8 us
    gather x8, local copies, waits for them, and re-layouts, score_block(): images = db_unit[slot_block]  39.8 us
    all_gather x1, waiting for transfers between devices, body(): gathered = lax.all_gather(query_unit, ('db', 'pb'), axis=0, tiled=True)  33.2 us
    dot_general x8, matrix products, score_block(): jnp.einsum('scq,skcd->skqd', group_block[:, 0], images, preferred_element...  32.1 us
    another operation x1, loops' own time, shard_scores(): return lax.map(score_block, starts).reshape(source_count, width)  14 us
    all_to_all x1, blocking collectives, body(): lax.all_to_all(found, ('db', 'pb'), split_axis=0, concat_axis=0, tiled=True)  10.4 us
    all_to_all x1, starting transfers between devices, body(): lax.all_to_all(requests, ('db', 'pb'), split_axis=1, concat_axis=1, tiled...  7.33 us
  transfers between devices with their start and end apart: 2, of which 1 were waited for; matrix products, arithmetic and copies ran while one was open for 8% of the time, Pallas kernels for 0%

commit v1 on v0

--- a/solution.py
+++ b/solution.py
@@ -8,6 +8,24 @@
 TOPK = 100
 epsilon = 1e-06
 score_scale = 8.0
+
+
+def in_order(blocks, dim):
+    blocks = jnp.moveaxis(blocks, 0, dim)
+    shape = blocks.shape
+    return blocks.reshape(*shape[:dim], shape[dim] * shape[dim + 1], *shape[dim + 2 :])
+
+
+def collected_by_bits(value, axis):
+    peers = lax.axis_size(axis)
+    blocks = value[None]
+    for level in range(peers.bit_length() - 1):
+        bit = 1 << level
+        other = lax.ppermute(blocks, axis, [(i, i ^ bit) for i in range(peers)])
+        both = jnp.stack([blocks, other])
+        upper = lax.axis_index(axis) >> level & 1
+        blocks = jnp.where(upper == 0, both, both[::-1]).reshape(-1, *value.shape)
+    return blocks
 
 
 def unit_maps(maps):
@@ -89,7 +107,7 @@
     send_slot = empty.at[shard_of, bucket_pos].set(slot_of)
     send_query = empty.at[shard_of, bucket_pos].set(query_of)
     requests = jnp.stack([send_slot, send_query])
-    gathered = lax.all_gather(query_unit, ("db", "pb"), axis=0, tiled=True)
+    gathered = in_order(collected_by_bits(query_unit, ("db", "pb")), 0)
     found = shard_scores(
         gathered,
         lax.all_to_all(requests, ("db", "pb"), split_axis=1, concat_axis=1, tiled=True)[0],

time: 319 us -> 343 us (1.075)
  waiting for transfers between devices: 33.2 us -> 59.7 us
  between operations: 14.2 us -> 0.9 us
  starting transfers between devices: 7.36 us -> 13.9 us
  other arithmetic: 14.3 us -> 18.5 us
    ppermute x0 -> x5, waiting for transfers between devices: none -> 40 us  [collected_by_bits(): other = lax.ppermute(blocks, axis, [(i, i ^ bit) for i in range(peers)])]
    all_gather x1 -> x0, waiting for transfers between devices: 33.2 us -> none  [body(): gathered = lax.all_gather(query_unit, ('db', 'pb'), axis=0, tiled=True)]
    all_to_all x1, waiting for transfers between devices: 0.01 us -> 19.7 us  [body(): lax.all_to_all(requests, ('db', 'pb'), split_axis=1, concat_axis=1, tiled...]
    ppermute x0 -> x5, starting transfers between devices: none -> 8.92 us  [collected_by_bits(): other = lax.ppermute(blocks, axis, [(i, i ^ bit) for i in range(peers)])]
    select_n x0 -> x4, other arithmetic: none -> 3.86 us  [collected_by_bits(): blocks = jnp.where(upper == 0, both, both[::-1]).reshape(-1, *value.shape)]
  transfers between devices with their start and end apart: 2 -> 6, of which waited for: 1 -> 5; matrix products, arithmetic and copies ran while one was open for 8% -> 6% of each run, Pallas kernels for 0% -> 0%
where the time goes in v1:
time: 343 us; the launch traced here: 341 us
  matrix products  160 us (47%)
  local copies, waits for them, and re-layouts  61.6 us (18%)
  waiting for transfers between devices  59.7 us (17%)
  other arithmetic  18.5 us (5%)
  loops' own time  14 us (4%)
  starting transfers between devices  13.9 us (4%)
  blocking collectives  12.7 us (4%)
    dot_general x8, matrix products, finish_pairs(): jnp.einsum('nqa,ba->nqb', rectified, conv_db, preferred_element_type=jnp....  69 us
    dot_general x8, matrix products, finish_pairs(): jnp.einsum('qa,nab->nqb', conv_query, rectified, preferred_element_type=j...  58.7 us
    ppermute x5, waiting for transfers between devices, collected_by_bits(): other = lax.ppermute(blocks, axis, [(i, i ^ bit) for i in range(peers)])  40 us
    gather x8, local copies, waits for them, and re-layouts, score_block(): images = db_unit[slot_block]  39.8 us
    dot_general x8, matrix products, score_block(): jnp.einsum('scq,skcd->skqd', group_block[:, 0], images, preferred_element...  32.1 us
    all_to_all x1, waiting for transfers between devices, body(): lax.all_to_all(requests, ('db', 'pb'), split_axis=1, concat_axis=1, tiled...  19.7 us
    another operation x1, loops' own time, shard_scores(): return lax.map(score_block, starts).reshape(source_count, width)  14 us
    all_to_all x1, blocking collectives, body(): lax.all_to_all(found, ('db', 'pb'), split_axis=0, concat_axis=0, tiled=True)  12.7 us
  transfers between devices with their start and end apart: 6, of which 5 were waited for; matrix products, arithmetic and copies ran while one was open for 6% of the time, Pallas kernels for 0%

profile of v1, /device:TPU:0, one launch (start us, length us, event | category | flops | bytes accessed | tf_op | source)
XLA Modules:
  0.0 341.0 jit_solution(12392830739413966655)
XLA Ops:
  12.1 11.2 %collective-permute-done.1 = bf16[2,1,256,256]{3,2,0,1:T(8,128)(2,1)S(1)} collective-permute-done((bf16[2,1,256,256]{3,2,0,1:T(8,128)(2,1)S(1)}, bf16[2,1,256,256]{3,2,0,1:T(8,128)(2,1)S(1)}, u32[]{:S(2)}, u32[]{:S(2)}) %collective-permute-start.1) | collective-permute-done | bytes 262176 | tf_op jit(solution)/shard_map/ppermute | solution.py:24
  27.7 23.3 %collective-permute-done.3 = bf16[8,1,256,256]{3,2,0,1:T(8,128)(2,1)S(1)} collective-permute-done((bf16[8,1,256,256]{3,2,0,1:T(8,128)(2,1)S(1)}, bf16[8,1,256,256]{3,2,0,1:T(8,128)(2,1)S(1)}, u32[]{:S(2)}, u32[]{:S(2)}) %collective-permute-start.3) | collective-permute-done | bytes 1048608 | tf_op jit(solution)/shard_map/ppermute | solution.py:24
  53.2 6.4 %scatter_fusion = s32[32,8]{0,1:T(8,128)S(1)} fusion(s32[32,8]{0,1:T(8,128)S(1)} %broadcast_in_dim.13.clone.1, s32[128]{0:T(128)S(1)} %fusion.64, s32[128]{0:T(128)S(1)} %get-tuple-element.431), kind=kCustom, calls=%fused_computation.2 | custom fusion | bytes 2560 | tf_op jit(solution)/shard_map/scatter | solution.py:107
  59.7 6.4 %scatter_fusion.1 = s32[32,8]{0,1:T(8,128)S(1)} fusion(s32[32,8]{0,1:T(8,128)S(1)} %broadcast_in_dim.13.clone, s32[128]{0:T(128)S(1)} %fusion.64, s32[128]{0:T(128)S(1)} %and_select_fusion.2), kind=kCustom, calls=%fused_computation.3 | custom fusion | bytes 2560 | tf_op jit(solution)/shard_map/scatter | solution.py:108
  66.8 5.0 %all-to-all-start = ((s32[2,32,8]{2,0,1:T(2,128)}), s32[2,32,8]{2,0,1:T(2,128)S(1)}, u32[]{:S(2)}, u32[]{:S(2)}) async-start(s32[2,32,8]{2,0,1:T(2,128)} %copy.26), calls=%async_computation | async-start | bytes 65536 | tf_op jit(solution)/shard_map/all_to_all | solution.py:113
  79.3 19.7 %all-to-all-done = s32[2,32,8]{2,0,1:T(2,128)S(1)} async-done(((s32[2,32,8]{2,0,1:T(2,128)}), s32[2,32,8]{2,0,1:T(2,128)S(1)}, u32[]{:S(2)}, u32[]{:S(2)}) %all-to-all-start) | async-done | bytes 2080 | tf_op jit(solution)/shard_map/all_to_all | solution.py:113
  104.1 220.1 %while.14 = (s32[]{:T(128)}, f32[8,32]{1,0:T(8,128)S(1)}, s32[8]{0:T(128)S(1)}, s32[32,8]{1,0:T(8,128)S(1)}, bf16[32,256,256]{2,1,0:T(8,128)(2,1)}, /*index=5*/b...) while((s32[]{:T(128)}, f32[8,32]{1,0:T(8,128)S(1)}, ...), condition=%wide.region_9.10_spmd.clone.clone, body=%wide.region_6.9_spmd.clone.clone.sunk | while | flops 3233940480 | bytes 42551080 | solution.py:81
  106.5 5.0 %gather_fusion = bf16[32,256,256]{2,1,0:T(8,128)(2,1)} fusion(bf16[32,256,256]{2,1,0:T(8,128)(2,1)} %get-tuple-element.692, s32[1024]{0:T(1024)S(1)} %pad_clamp_fusion.2), kind=kCustom, calls=%fused_computation.clone.clone.clone.1 | custom fusion | bytes 8388736 | tf_op jit(solution)/shard_map/while/body/eval_jaxpr/gather | solution.py:71
  115.5 7.3 %fusion.85 = f32[32,256,256]{1,2,0:T(8,128)S(1)} fusion(bf16[32,256,256]{1,2,0:T(8,128)(2,1)S(1)} %bitcast.145, f32[]{:T(128)} %get-tuple-element.708, f32[]{:T(128)} %get-tuple-element.705, f32[]{:T(128)} %get-tuple-element.703, f32[]{:T(128)} %get-tuple-element.701, f32[]{:T(128)} %get-tuple-element.699, f32[]{:T(128)} %get-tuple-element.698, ...), kind=kOutput, calls=%fused_computation.23.clone.1 | convolution fusion | flops 1075904512 | bytes 12589092 | tf_op jit(solution)/shard_map/while/body/eval_jaxpr/qa,nab->nqb/dot_general | solution.py:55
  122.9 8.6 %fusion.86 = f32[32,256]{1,0:T(8,128)S(1)} fusion(f32[32,256,256]{1,2,0:T(8,128)S(1)} %fusion.85, bf16[32,256,256]{1,2,0:T(8,128)(2,1)S(1)} %bitcast.146, f32[]{:T(128)} %get-tuple-element.717, f32[]{:T(128)} %get-tuple-element.716, f32[]{:T(128)} %get-tuple-element.715, f32[]{:T(128)} %get-tuple-element.714, f32[]{:T(128)} %get-tuple-element.713, ...), kind=kOutput, calls=%fused_computation.7.clone.1 | convolution fusion | flops 1080090624 | bytes 12621860 | tf_op jit(solution)/shard_map/while/body/eval_jaxpr/nqa,ba->nqb/dot_general | solution.py:56
  134.0 5.0 %gather_fusion = bf16[32,256,256]{2,1,0:T(8,128)(2,1)} fusion(bf16[32,256,256]{2,1,0:T(8,128)(2,1)} %get-tuple-element.692, s32[1024]{0:T(1024)S(1)} %pad_clamp_fusion.2), kind=kCustom, calls=%fused_computation.clone.clone.clone.1 | custom fusion | bytes 8388736 | tf_op jit(solution)/shard_map/while/body/eval_jaxpr/gather | solution.py:71
  143.0 7.3 %fusion.85 = f32[32,256,256]{1,2,0:T(8,128)S(1)} fusion(bf16[32,256,256]{1,2,0:T(8,128)(2,1)S(1)} %bitcast.145, f32[]{:T(128)} %get-tuple-element.708, f32[]{:T(128)} %get-tuple-element.705, f32[]{:T(128)} %get-tuple-element.703, f32[]{:T(128)} %get-tuple-element.701, f32[]{:T(128)} %get-tuple-element.699, f32[]{:T(128)} %get-tuple-element.698, ...), kind=kOutput, calls=%fused_computation.23.clone.1 | convolution fusion | flops 1075904512 | bytes 12589092 | tf_op jit(solution)/shard_map/while/body/eval_jaxpr/qa,nab->nqb/dot_general | solution.py:55
  150.4 8.6 %fusion.86 = f32[32,256]{1,0:T(8,128)S(1)} fusion(f32[32,256,256]{1,2,0:T(8,128)S(1)} %fusion.85, bf16[32,256,256]{1,2,0:T(8,128)(2,1)S(1)} %bitcast.146, f32[]{:T(128)} %get-tuple-element.717, f32[]{:T(128)} %get-tuple-element.716, f32[]{:T(128)} %get-tuple-element.715, f32[]{:T(128)} %get-tuple-element.714, f32[]{:T(128)} %get-tuple-element.713, ...), kind=kOutput, calls=%fused_computation.7.clone.1 | convolution fusion | flops 1080090624 | bytes 12621860 | tf_op jit(solution)/shard_map/while/body/eval_jaxpr/nqa,ba->nqb/dot_general | solution.py:56
  161.6 5.0 %gather_fusion = bf16[32,256,256]{2,1,0:T(8,128)(2,1)} fusion(bf16[32,256,256]{2,1,0:T(8,128)(2,1)} %get-tuple-element.692, s32[1024]{0:T(1024)S(1)} %pad_clamp_fusion.2), kind=kCustom, calls=%fused_computation.clone.clone.clone.1 | custom fusion | bytes 8388736 | tf_op jit(solution)/shard_map/while/body/eval_jaxpr/gather | solution.py:71
  170.6 7.3 %fusion.85 = f32[32,256,256]{1,2,0:T(8,128)S(1)} fusion(bf16[32,256,256]{1,2,0:T(8,128)(2,1)S(1)} %bitcast.145, f32[]{:T(128)} %get-tuple-element.708, f32[]{:T(128)} %get-tuple-element.705, f32[]{:T(128)} %get-tuple-element.703, f32[]{:T(128)} %get-tuple-element.701, f32[]{:T(128)} %get-tuple-element.699, f32[]{:T(128)} %get-tuple-element.698, ...), kind=kOutput, calls=%fused_computation.23.clone.1 | convolution fusion | flops 1075904512 | bytes 12589092 | tf_op jit(solution)/shard_map/while/body/eval_jaxpr/qa,nab->nqb/dot_general | solution.py:55
  177.9 8.6 %fusion.86 = f32[32,256]{1,0:T(8,128)S(1)} fusion(f32[32,256,256]{1,2,0:T(8,128)S(1)} %fusion.85, bf16[32,256,256]{1,2,0:T(8,128)(2,1)S(1)} %bitcast.146, f32[]{:T(128)} %get-tuple-element.717, f32[]{:T(128)} %get-tuple-element.716, f32[]{:T(128)} %get-tuple-element.715, f32[]{:T(128)} %get-tuple-element.714, f32[]{:T(128)} %get-tuple-element.713, ...), kind=kOutput, calls=%fused_computation.7.clone.1 | convolution fusion | flops 1080090624 | bytes 12621860 | tf_op jit(solution)/shard_map/while/body/eval_jaxpr/nqa,ba->nqb/dot_general | solution.py:56
  189.1 5.0 %gather_fusion = bf16[32,256,256]{2,1,0:T(8,128)(2,1)} fusion(bf16[32,256,256]{2,1,0:T(8,128)(2,1)} %get-tuple-element.692, s32[1024]{0:T(1024)S(1)} %pad_clamp_fusion.2), kind=kCustom, calls=%fused_computation.clone.clone.clone.1 | custom fusion | bytes 8388736 | tf_op jit(solution)/shard_map/while/body/eval_jaxpr/gather | solution.py:71
  198.1 7.3 %fusion.85 = f32[32,256,256]{1,2,0:T(8,128)S(1)} fusion(bf16[32,256,256]{1,2,0:T(8,128)(2,1)S(1)} %bitcast.145, f32[]{:T(128)} %get-tuple-element.708, f32[]{:T(128)} %get-tuple-element.705, f32[]{:T(128)} %get-tuple-element.703, f32[]{:T(128)} %get-tuple-element.701, f32[]{:T(128)} %get-tuple-element.699, f32[]{:T(128)} %get-tuple-element.698, ...), kind=kOutput, calls=%fused_computation.23.clone.1 | convolution fusion | flops 1075904512 | bytes 12589092 | tf_op jit(solution)/shard_map/while/body/eval_jaxpr/qa,nab->nqb/dot_general | solution.py:55
  205.4 8.6 %fusion.86 = f32[32,256]{1,0:T(8,128)S(1)} fusion(f32[32,256,256]{1,2,0:T(8,128)S(1)} %fusion.85, bf16[32,256,256]{1,2,0:T(8,128)(2,1)S(1)} %bitcast.146, f32[]{:T(128)} %get-tuple-element.717, f32[]{:T(128)} %get-tuple-element.716, f32[]{:T(128)} %get-tuple-element.715, f32[]{:T(128)} %get-tuple-element.714, f32[]{:T(128)} %get-tuple-element.713, ...), kind=kOutput, calls=%fused_computation.7.clone.1 | convolution fusion | flops 1080090624 | bytes 12621860 | tf_op jit(solution)/shard_map/while/body/eval_jaxpr/nqa,ba->nqb/dot_general | solution.py:56
  216.6 5.0 %gather_fusion = bf16[32,256,256]{2,1,0:T(8,128)(2,1)} fusion(bf16[32,256,256]{2,1,0:T(8,128)(2,1)} %get-tuple-element.692, s32[1024]{0:T(1024)S(1)} %pad_clamp_fusion.2), kind=kCustom, calls=%fused_computation.clone.clone.clone.1 | custom fusion | bytes 8388736 | tf_op jit(solution)/shard_map/while/body/eval_jaxpr/gather | solution.py:71
  225.6 7.3 %fusion.85 = f32[32,256,256]{1,2,0:T(8,128)S(1)} fusion(bf16[32,256,256]{1,2,0:T(8,128)(2,1)S(1)} %bitcast.145, f32[]{:T(128)} %get-tuple-element.708, f32[]{:T(128)} %get-tuple-element.705, f32[]{:T(128)} %get-tuple-element.703, f32[]{:T(128)} %get-tuple-element.701, f32[]{:T(128)} %get-tuple-element.699, f32[]{:T(128)} %get-tuple-element.698, ...), kind=kOutput, calls=%fused_computation.23.clone.1 | convolution fusion | flops 1075904512 | bytes 12589092 | tf_op jit(solution)/shard_map/while/body/eval_jaxpr/qa,nab->nqb/dot_general | solution.py:55
  232.9 8.6 %fusion.86 = f32[32,256]{1,0:T(8,128)S(1)} fusion(f32[32,256,256]{1,2,0:T(8,128)S(1)} %fusion.85, bf16[32,256,256]{1,2,0:T(8,128)(2,1)S(1)} %bitcast.146, f32[]{:T(128)} %get-tuple-element.717, f32[]{:T(128)} %get-tuple-element.716, f32[]{:T(128)} %get-tuple-element.715, f32[]{:T(128)} %get-tuple-element.714, f32[]{:T(128)} %get-tuple-element.713, ...), kind=kOutput, calls=%fused_computation.7.clone.1 | convolution fusion | flops 1080090624 | bytes 12621860 | tf_op jit(solution)/shard_map/while/body/eval_jaxpr/nqa,ba->nqb/dot_general | solution.py:56
  244.1 5.0 %gather_fusion = bf16[32,256,256]{2,1,0:T(8,128)(2,1)} fusion(bf16[32,256,256]{2,1,0:T(8,128)(2,1)} %get-tuple-element.692, s32[1024]{0:T(1024)S(1)} %pad_clamp_fusion.2), kind=kCustom, calls=%fused_computation.clone.clone.clone.1 | custom fusion | bytes 8388736 | tf_op jit(solution)/shard_map/while/body/eval_jaxpr/gather | solution.py:71
  253.1 7.3 %fusion.85 = f32[32,256,256]{1,2,0:T(8,128)S(1)} fusion(bf16[32,256,256]{1,2,0:T(8,128)(2,1)S(1)} %bitcast.145, f32[]{:T(128)} %get-tuple-element.708, f32[]{:T(128)} %get-tuple-element.705, f32[]{:T(128)} %get-tuple-element.703, f32[]{:T(128)} %get-tuple-element.701, f32[]{:T(128)} %get-tuple-element.699, f32[]{:T(128)} %get-tuple-element.698, ...), kind=kOutput, calls=%fused_computation.23.clone.1 | convolution fusion | flops 1075904512 | bytes 12589092 | tf_op jit(solution)/shard_map/while/body/eval_jaxpr/qa,nab->nqb/dot_general | solution.py:55
  260.5 8.6 %fusion.86 = f32[32,256]{1,0:T(8,128)S(1)} fusion(f32[32,256,256]{1,2,0:T(8,128)S(1)} %fusion.85, bf16[32,256,256]{1,2,0:T(8,128)(2,1)S(1)} %bitcast.146, f32[]{:T(128)} %get-tuple-element.717, f32[]{:T(128)} %get-tuple-element.716, f32[]{:T(128)} %get-tuple-element.715, f32[]{:T(128)} %get-tuple-element.714, f32[]{:T(128)} %get-tuple-element.713, ...), kind=kOutput, calls=%fused_computation.7.clone.1 | convolution fusion | flops 1080090624 | bytes 12621860 | tf_op jit(solution)/shard_map/while/body/eval_jaxpr/nqa,ba->nqb/dot_general | solution.py:56
  271.6 5.0 %gather_fusion = bf16[32,256,256]{2,1,0:T(8,128)(2,1)} fusion(bf16[32,256,256]{2,1,0:T(8,128)(2,1)} %get-tuple-element.692, s32[1024]{0:T(1024)S(1)} %pad_clamp_fusion.2), kind=kCustom, calls=%fused_computation.clone.clone.clone.1 | custom fusion | bytes 8388736 | tf_op jit(solution)/shard_map/while/body/eval_jaxpr/gather | solution.py:71
  280.6 7.3 %fusion.85 = f32[32,256,256]{1,2,0:T(8,128)S(1)} fusion(bf16[32,256,256]{1,2,0:T(8,128)(2,1)S(1)} %bitcast.145, f32[]{:T(128)} %get-tuple-element.708, f32[]{:T(128)} %get-tuple-element.705, f32[]{:T(128)} %get-tuple-element.703, f32[]{:T(128)} %get-tuple-element.701, f32[]{:T(128)} %get-tuple-element.699, f32[]{:T(128)} %get-tuple-element.698, ...), kind=kOutput, calls=%fused_computation.23.clone.1 | convolution fusion | flops 1075904512 | bytes 12589092 | tf_op jit(solution)/shard_map/while/body/eval_jaxpr/qa,nab->nqb/dot_general | solution.py:55
  288.0 8.6 %fusion.86 = f32[32,256]{1,0:T(8,128)S(1)} fusion(f32[32,256,256]{1,2,0:T(8,128)S(1)} %fusion.85, bf16[32,256,256]{1,2,0:T(8,128)(2,1)S(1)} %bitcast.146, f32[]{:T(128)} %get-tuple-element.717, f32[]{:T(128)} %get-tuple-element.716, f32[]{:T(128)} %get-tuple-element.715, f32[]{:T(128)} %get-tuple-element.714, f32[]{:T(128)} %get-tuple-element.713, ...), kind=kOutput, calls=%fused_computation.7.clone.1 | convolution fusion | flops 1080090624 | bytes 12621860 | tf_op jit(solution)/shard_map/while/body/eval_jaxpr/nqa,ba->nqb/dot_general | solution.py:56
  299.2 5.0 %gather_fusion = bf16[32,256,256]{2,1,0:T(8,128)(2,1)} fusion(bf16[32,256,256]{2,1,0:T(8,128)(2,1)} %get-tuple-element.692, s32[1024]{0:T(1024)S(1)} %pad_clamp_fusion.2), kind=kCustom, calls=%fused_computation.clone.clone.clone.1 | custom fusion | bytes 8388736 | tf_op jit(solution)/shard_map/while/body/eval_jaxpr/gather | solution.py:71
  308.2 7.3 %fusion.85 = f32[32,256,256]{1,2,0:T(8,128)S(1)} fusion(bf16[32,256,256]{1,2,0:T(8,128)(2,1)S(1)} %bitcast.145, f32[]{:T(128)} %get-tuple-element.708, f32[]{:T(128)} %get-tuple-element.705, f32[]{:T(128)} %get-tuple-element.703, f32[]{:T(128)} %get-tuple-element.701, f32[]{:T(128)} %get-tuple-element.699, f32[]{:T(128)} %get-tuple-element.698, ...), kind=kOutput, calls=%fused_computation.23.clone.1 | convolution fusion | flops 1075904512 | bytes 12589092 | tf_op jit(solution)/shard_map/while/body/eval_jaxpr/qa,nab->nqb/dot_general | solution.py:55
  315.5 8.6 %fusion.86 = f32[32,256]{1,0:T(8,128)S(1)} fusion(f32[32,256,256]{1,2,0:T(8,128)S(1)} %fusion.85, bf16[32,256,256]{1,2,0:T(8,128)(2,1)S(1)} %bitcast.146, f32[]{:T(128)} %get-tuple-element.717, f32[]{:T(128)} %get-tuple-element.716, f32[]{:T(128)} %get-tuple-element.715, f32[]{:T(128)} %get-tuple-element.714, f32[]{:T(128)} %get-tuple-element.713, ...), kind=kOutput, calls=%fused_computation.7.clone.1 | convolution fusion | flops 1080090624 | bytes 12621860 | tf_op jit(solution)/shard_map/while/body/eval_jaxpr/nqa,ba->nqb/dot_general | solution.py:56
  324.4 12.7 %all_to_all.17 = f32[32,1,8]{2,1,0:T(1,128)S(1)} all-to-all(f32[32,1,8]{2,1,0:T(1,128)S(1)} %bitcast.162), channel_id=1, replica_groups=mesh['db'=8,'pb'=4] {'db','pb'}, dimensions={0} | all-to-all | bytes 2048 | tf_op jit(solution)/shard_map/all_to_all | solution.py:118
  (121 shorter events, 73.8 us)
Async XLA Ops:
  0.6 26.6 %copy-start.3 = (s32[1,128]{1,0:T(1,128)S(1)}, s32[1,128]{1,0:T(1,128)}, u32[]{:S(2)}) copy-start(s32[1,128]{1,0:T(1,128)} %param.9) | copy-start | bytes 1540
  2.5 6.6 %collective-permute-start = (bf16[1,1,256,256]{3,2,1,0:T(8,128)(2,1)S(1)}, bf16[1,1,256,256]{3,2,1,0:T(8,128)(2,1)S(1)}, u32[]{:S(2)}, u32[]{:S(2)}) collective-permute-start(bf16[1,1,256,256]{3,2,1,0:T(8,128)(2,1)S(1)} %get-tuple-element.412), channel_id=1, source_target_pairs={{0,1},{1,0},{2,3},{3,2},{4,5},{5,4},{6,7},{7,6},{8,9},{9,8},{10,11... | collective-permute-start | bytes 393224 | tf_op jit(solution)/shard_map/ppermute | solution.py:24
  9.3 14.1 %collective-permute-start.1 = (bf16[2,1,256,256]{3,2,0,1:T(8,128)(2,1)S(1)}, bf16[2,1,256,256]{3,2,0,1:T(8,128)(2,1)S(1)}, u32[]{:S(2)}, u32[]{:S(2)}) collective-permute-start(bf16[2,1,256,256]{3,2,0,1:T(8,128)(2,1)S(1)} %get-tuple-element.410), channel_id=1, source_target_pairs={{0,2},{1,3},{2,0},{3,1},{4,6},{5,7},{6,4},{7,5},{8,10},{9,11},{10,... | collective-permute-start | bytes 786440 | tf_op jit(solution)/shard_map/ppermute | solution.py:24
  23.5 2.0 collective-permute-start.2
  25.7 25.3 %collective-permute-start.3 = (bf16[8,1,256,256]{3,2,0,1:T(8,128)(2,1)S(1)}, bf16[8,1,256,256]{3,2,0,1:T(8,128)(2,1)S(1)}, u32[]{:S(2)}, u32[]{:S(2)}) collective-permute-start(bf16[8,1,256,256]{3,2,0,1:T(8,128)(2,1)S(1)} %bitcast.154), channel_id=1, source_target_pairs={{0,8},{1,9},{2,10},{3,11},{4,12},{5,13},{6,14},{7,15},{8,0},{9,1},... | collective-permute-start | bytes 3145736 | tf_op jit(solution)/shard_map/ppermute | solution.py:24
  51.2 20.6 %copy-start.1 = (bf16[3,3]{1,0:T(4,128)(2,1)S(1)}, bf16[3,3]{1,0:T(4,128)(2,1)}, u32[]{:S(2)}) copy-start(bf16[3,3]{1,0:T(4,128)(2,1)} %param.10) | copy-start | bytes 58
  51.2 21.3 %copy-start.2 = (bf16[3,3]{1,0:T(4,128)(2,1)S(1)}, bf16[3,3]{1,0:T(4,128)(2,1)}, u32[]{:S(2)}) copy-start(bf16[3,3]{1,0:T(4,128)(2,1)} %param.11) | copy-start | bytes 58
  51.7 47.3 %collective-permute-start.4 = (bf16[16,1,256,256]{3,2,0,1:T(8,128)(2,1)S(1)}, bf16[16,1,256,256]{3,2,0,1:T(8,128)(2,1)}, u32[]{:S(2)}, u32[]{:S(2)}) collective-permute-start(bf16[16,1,256,256]{3,2,0,1:T(8,128)(2,1)S(1)} %bitcast.152), channel_id=1, source_target_pairs={{0,16},{1,17},{2,18},{3,19},{4,20},{5,21},{6,22},{7,23},{8,24},{9,... | collective-permute-start | bytes 6291464 | tf_op jit(solution)/shard_map/ppermute | solution.py:24
  66.8 32.2 %all-to-all-start = ((s32[2,32,8]{2,0,1:T(2,128)}), s32[2,32,8]{2,0,1:T(2,128)S(1)}, u32[]{:S(2)}, u32[]{:S(2)}) async-start(s32[2,32,8]{2,0,1:T(2,128)} %copy.26), calls=%async_computation | async-start | bytes 65536 | tf_op jit(solution)/shard_map/all_to_all | solution.py:113
  71.8 4.5 %copy-start = (bf16[32,256,256]{2,1,0:T(8,128)(2,1)S(1)}, bf16[32,256,256]{2,1,0:T(8,128)(2,1)}, u32[]{:S(2)}) copy-start(bf16[32,256,256]{2,1,0:T(8,128)(2,1)} %param.8) | copy-start | bytes 12582916
  338.3 2.7 copy-start.4
